TPU v7x, 128 devices: a whole 4x4x4 slice. The times are simulated.
128 devices in a mesh: segment: 4 (over x_lo, core), fsdp: 8 (over z, x_hi), dp: 4 (over y).
Axes of the slice: x: 4 (x_hi: 2, x_lo: 2; x = x_hi * 2 + x_lo), y: 4, z: 4, core: 2. Of those that a mesh axis runs over, the one named last changes fastest.
Arguments:
- inputs: bfloat16 [3, 64, 49, 2880], P(None, ('fsdp', 'dp')), may hold values from -6 to 6
- cotangent: bfloat16 [3, 64, 49, 2880], P(None, ('fsdp', 'dp')), may hold values from -0.119628906 to 0.119628906
- plan: int32 [3], replicated, may hold values from 0 to 2, each once
- weight: bfloat16 [4, 2880, 2880], P('segment', 'fsdp'), may hold values from -0.109375 to 0.109375
- squeeze: bfloat16 [4, 2880, 360], P('segment', 'fsdp'), may hold values from -0.109375 to 0.109375
- excite: bfloat16 [4, 2880, 360], P('segment', 'fsdp'), may hold values from -0.3125 to 0.3125
Outputs:
- grad_weight: float32 [4, 2880, 2880], P('segment', ('fsdp', 'dp'))
- grad_squeeze: float32 [4, 2880, 360], P('segment', ('fsdp', 'dp'))
- grad_excite: float32 [4, 2880, 360], P('segment', ('fsdp', 'dp'))
Inputs may be any that keep to these rules, and one draw needn't show every extreme that they name: plan names each of the 3 microbatches exactly once.
All inputs are finite; a program needn't handle non-finite values.
Results may differ from a plain program's by a relative error of at most 0.024.
Values may be sent and summed in bfloat16 or wider, within the bound.
A program may use at most 128 MiB of HBM per device.

v0:
```python
import jax
import jax.numpy as jnp
from jax import lax
from jax.sharding import PartitionSpec as P


def shifted(value, axis, steps):
    count = lax.axis_size(axis)
    leading, last = (max(0, -steps), min(count, count - steps))
    return lax.ppermute(value, axis, [(source, source + steps) for source in range(leading, last)])


def silu_slope(value):
    sigma = jax.nn.sigmoid(value)
    return sigma * (1.0 + value * (1.0 - sigma))


def contract_rows(left, right):
    return lax.dot_general(
        left, right, (((0,), (0,)), ((), ())), preferred_element_type=jnp.float32
    )


def contract_cols(left, right):
    return lax.dot_general(
        left, right, (((1,), (1,)), ((), ())), preferred_element_type=jnp.float32
    )


def project(images, matrix):
    flat = images.reshape(-1, images.shape[-1])
    result = jnp.dot(flat, matrix, preferred_element_type=jnp.float32)
    return result.reshape(images.shape[:-1] + (matrix.shape[1],))


def forward_block(images, matrix, squeeze_w, excite_w):
    pre = project(images, matrix)
    active_map = jax.nn.silu(pre).astype(jnp.bfloat16)
    pooled = jnp.mean(active_map.astype(jnp.float32), axis=1).astype(jnp.bfloat16)
    squeezed = jnp.dot(pooled, squeeze_w, preferred_element_type=jnp.float32)
    hidden = jax.nn.silu(squeezed).astype(jnp.bfloat16)
    gate = jax.nn.sigmoid(contract_cols(hidden, excite_w))
    output = (
        images.astype(jnp.float32) + active_map.astype(jnp.float32) * gate[:, None, :]
    ).astype(jnp.bfloat16)
    return (output, pre, pooled, squeezed, hidden, gate)


def backward_block(images, pre, squeezed, gate, upstream, matrix, squeeze_w, excite_w):
    active_map = jax.nn.silu(pre).astype(jnp.bfloat16)
    upper = upstream.astype(jnp.float32)
    d_act = upper * gate[:, None, :]
    d_gate = jnp.sum(upper * active_map.astype(jnp.float32), axis=1)
    d_excite = (d_gate * gate * (1.0 - gate)).astype(jnp.bfloat16)
    d_hidden = jnp.dot(d_excite, excite_w, preferred_element_type=jnp.float32)
    d_squeezed = (d_hidden * silu_slope(squeezed)).astype(jnp.bfloat16)
    d_pooled = contract_cols(d_squeezed, squeeze_w)
    d_act = d_act + d_pooled[:, None, :] / images.shape[1]
    d_pre = (d_act * silu_slope(pre)).astype(jnp.bfloat16)
    flat = d_pre.reshape(-1, d_pre.shape[-1])
    back = contract_cols(flat, matrix).reshape(images.shape)
    d_images = (upper + back).astype(jnp.bfloat16)
    return (d_excite, d_squeezed, d_pre, d_images)


def put_slot(store, position, value, active):
    current = lax.dynamic_index_in_dim(store, position, 0, keepdims=False)
    return lax.dynamic_update_index_in_dim(store, jnp.where(active, value, current), position, 0)


def take_slot(store, position):
    return lax.dynamic_index_in_dim(store, position, 0, keepdims=False)


def on_device(inputs, cotangent, plan, weight, squeeze, excite):
    full_w, full_s, full_e = (
        lax.all_gather(weight[0], "fsdp", axis=0, tiled=True),
        lax.all_gather(squeeze[0], "fsdp", axis=0, tiled=True),
        lax.all_gather(excite[0], "fsdp", axis=0, tiled=True),
    )
    sections = lax.axis_size("segment")
    segment_id = lax.axis_index("segment")
    ordered = inputs[plan]
    micro, images, pixels, width = ordered.shape
    hidden_width = full_s.shape[1]
    steps_total = micro + sections - 1
    store_in = jnp.zeros((micro, images, pixels, width), jnp.bfloat16)
    store_pre = jnp.zeros((micro, images, pixels, width), jnp.float32)
    store_pool = jnp.zeros((micro, images, width), jnp.bfloat16)
    store_sq = jnp.zeros((micro, images, hidden_width), jnp.float32)
    store_hid = jnp.zeros((micro, images, hidden_width), jnp.bfloat16)
    store_gate = jnp.zeros((micro, images, width), jnp.float32)
    incoming = jnp.zeros((images, pixels, width), jnp.bfloat16)
    for step in range(steps_total):
        slot_now = step - segment_id
        active = (slot_now >= 0) & (slot_now < micro)
        position = jnp.clip(slot_now, 0, micro - 1)
        first_in = ordered[min(step, micro - 1)]
        images_in = jnp.where(segment_id == 0, first_in, incoming)
        output, pre, pooled, squeezed, hidden, gate = forward_block(
            images_in, full_w, full_s, full_e
        )
        store_in = put_slot(store_in, position, images_in, active)
        store_pre = put_slot(store_pre, position, pre, active)
        store_pool = put_slot(store_pool, position, pooled, active)
        store_sq = put_slot(store_sq, position, squeezed, active)
        store_hid = put_slot(store_hid, position, hidden, active)
        store_gate = put_slot(store_gate, position, gate, active)
        if step < steps_total - 1:
            incoming = shifted(output, "segment", 1)
    store_dpre = jnp.zeros((micro, images, pixels, width), jnp.bfloat16)
    store_dsq = jnp.zeros((micro, images, hidden_width), jnp.bfloat16)
    store_dex = jnp.zeros((micro, images, width), jnp.bfloat16)
    incoming_grad = jnp.zeros((images, pixels, width), jnp.bfloat16)
    for step in range(steps_total):
        slot_now = micro - 1 - step + (sections - 1 - segment_id)
        active = (slot_now >= 0) & (slot_now < micro)
        position = jnp.clip(slot_now, 0, micro - 1)
        last_in = cotangent[max(micro - 1 - step, 0)]
        upstream = jnp.where(segment_id == sections - 1, last_in, incoming_grad)
        images_in = take_slot(store_in, position)
        pre = take_slot(store_pre, position)
        squeezed = take_slot(store_sq, position)
        gate = take_slot(store_gate, position)
        d_excite, d_squeezed, d_pre, d_images = backward_block(
            images_in, pre, squeezed, gate, upstream, full_w, full_s, full_e
        )
        store_dpre = put_slot(store_dpre, position, d_pre, active)
        store_dsq = put_slot(store_dsq, position, d_squeezed, active)
        store_dex = put_slot(store_dex, position, d_excite, active)
        if step < steps_total - 1:
            incoming_grad = shifted(d_images, "segment", -1)
    flat_in = store_in.reshape(-1, width)
    flat_dpre = store_dpre.reshape(-1, width)
    grad_s = contract_rows(store_pool.reshape(-1, width), store_dsq.reshape(-1, hidden_width))
    grad_e = contract_rows(store_dex.reshape(-1, width), store_hid.reshape(-1, hidden_width))
    grad_w = contract_rows(flat_in, flat_dpre)
    shard_w, shard_s, shard_e = (
        lax.psum_scatter(
            grad_w.astype(jnp.bfloat16), ("fsdp", "dp"), scatter_dimension=0, tiled=True
        ).astype(jnp.float32),
        lax.psum_scatter(
            grad_s.astype(jnp.bfloat16), ("fsdp", "dp"), scatter_dimension=0, tiled=True
        ).astype(jnp.float32),
        lax.psum_scatter(
            grad_e.astype(jnp.bfloat16), ("fsdp", "dp"), scatter_dimension=0, tiled=True
        ).astype(jnp.float32),
    )
    return (shard_w[None], shard_s[None], shard_e[None])


def solution(mesh):
    placed = (
        P(None, ("fsdp", "dp"), None, None),
        P(None, ("fsdp", "dp"), None, None),
        P(),
        P("segment", "fsdp", None),
        P("segment", "fsdp", None),
        P("segment", "fsdp", None),
    )
    return jax.shard_map(
        on_device,
        mesh=mesh,
        in_specs=placed,
        out_specs=(
            P("segment", ("fsdp", "dp"), None),
            P("segment", ("fsdp", "dp"), None),
            P("segment", ("fsdp", "dp"), None),
        ),
        check_vma=False,
    )
```

profile of v0, /device:TPU:42, one launch (start us, length us, event | category | flops | bytes accessed | tf_op | source)
XLA Modules:
  0.0 888.8 jit_solution(14493084215448957604)
XLA Ops:
  9.5 6.0 gather_fusion
  15.4 3.4 fusion.357
  25.6 168.4 %all-gather.7.cloned.1.call-done = bf16[1,2880,2880]{2,1,0:T(8,128)(2,1)} async-done(((bf16[1,360,2880]{2,1,0:T(8,128)(2,1)}), bf16[1,2880,2880]{2,1,0:T(8,128)(2,1)}) %all-gather.7.cloned.1.call-update) | async-done | bytes 16588816 | tf_op jit(solution)/shard_map/all_gather | solution.py:77
  194.0 9.7 %convert_reduce_fusion.4 = (f32[2,2880]{1,0:T(2,128)S(1)}, bf16[2,49,2880]{2,1,0:T(8,128)(2,1)S(1)}, f32[2,49,2880]{2,1,0:T(8,128)}) fusion(bf16[1,2880,2880]{2,1,0:T(8,128)(2,1)} %all-gather.7.cloned.1.call-done, bf16[1,2,49,2880]{3,1,2,0:T(2,128)(2,1)S(1)} %get-tuple-element.33, pred[]{:T(512)S(6)} %eq.4), kind=kOutput, calls=%fused_computation.130 | convolution fusion | flops 1627954560 | bytes 18869760 | tf_op jit(solution)/shard_map/dot_general | solution.py:32
  203.7 45.0 %all-gather.9.cloned.1.call-done = bf16[1,2880,360]{2,1,0:T(8,128)(2,1)} async-done(((bf16[1,360,360]{2,1,0:T(8,128)(2,1)}), bf16[1,2880,360]{2,1,0:T(8,128)(2,1)}) %all-gather.9.cloned.1.call-update) | async-done | bytes 2073616 | tf_op jit(solution)/shard_map/all_gather | solution.py:78
  250.7 52.7 %all-gather.11.cloned.1.call-done = bf16[1,2880,360]{2,1,0:T(8,128)(2,1)} async-done(((bf16[1,360,360]{2,1,0:T(8,128)(2,1)}), bf16[1,2880,360]{2,1,0:T(8,128)(2,1)}) %all-gather.11.cloned.1.call-update) | async-done | bytes 2073616 | tf_op jit(solution)/shard_map/all_gather | solution.py:79
  310.5 7.0 collective-permute-done
  317.5 8.8 convert_reduce_fusion.3
  335.2 5.6 collective-permute-done.1
  340.8 4.0 convert_reduce_fusion.2
  351.4 6.4 collective-permute-done.2
  357.8 4.0 convert_reduce_fusion.1
  368.2 6.6 collective-permute-done.3
  385.1 5.9 collective-permute-done.4
  391.0 5.0 bitcast_dynamic-update-slice_fusion
  396.0 3.2 fusion.126
  404.0 12.6 %fusion.54 = bf16[2,49,2880]{2,1,0:T(8,128)(2,1)} fusion(bf16[1,2880,2880]{2,1,0:T(8,128)(2,1)} %all-gather.7.cloned.1.call-done, f32[3,2,49,2880]{3,2,1,0:T(8,128)} %copy-done.9, s32[]{:T(128)S(6)} %min.30, f32[2,2880]{1,0:T(2,128)} %convolution_multiply_fusion.5, f32[2,2880]{1,0:T(2,128)} %copy-done.39, bf16[1,2,49,2880]{3,1,2,0:T(2,128)(2,1)} %get-tuple-element.30, ...), kind=kOutput, calls=%fused_computation.37 | convolution fusion | flops 1630500480 | bytes 20043520 | tf_op jit(solution)/shard_map/dot_general | solution.py:25
  431.9 12.4 %fusion.51 = bf16[2,49,2880]{2,1,0:T(8,128)(2,1)} fusion(bf16[1,2880,2880]{2,1,0:T(8,128)(2,1)} %all-gather.7.cloned.1.call-done, bf16[2,49,2880]{2,0,1:T(2,128)(2,1)} %copy-done.24, bf16[1,2,49,2880]{3,1,2,0:T(2,128)(2,1)S(1)} %copy-done.14, pred[]{:T(512)S(6)} %eq.5, f32[3,2,49,2880]{3,2,1,0:T(8,128)} %copy-done.9, s32[]{:T(128)S(6)} %min.29, ...), kind=kOutput, calls=%fused_computation.36 | convolution fusion | flops 1630500480 | bytes 21197568 | tf_op jit(solution)/shard_map/dot_general | solution.py:25
  445.9 4.1 collective-permute-start.6
  461.2 12.2 %fusion.48 = bf16[2,49,2880]{2,1,0:T(8,128)(2,1)} fusion(bf16[1,2880,2880]{2,1,0:T(8,128)(2,1)} %all-gather.7.cloned.1.call-done, bf16[2,49,2880]{2,0,1:T(2,128)(2,1)S(1)} %copy-done.27, bf16[1,2,49,2880]{3,1,2,0:T(2,128)(2,1)S(1)} %get-tuple-element.28, pred[]{:T(512)S(6)} %eq.5, f32[3,2,49,2880]{3,2,1,0:T(8,128)} %copy-done.9, s32[]{:T(128)S(6)} %min.28, ...), kind=kOutput, calls=%fused_computation.35 | convolution fusion | flops 1630500480 | bytes 21197568 | tf_op jit(solution)/shard_map/dot_general | solution.py:25
  475.0 4.0 collective-permute-start.7
  490.4 12.2 %fusion.45 = bf16[2,49,2880]{2,1,0:T(8,128)(2,1)} fusion(bf16[1,2880,2880]{2,1,0:T(8,128)(2,1)} %all-gather.7.cloned.1.call-done, bf16[2,49,2880]{2,0,1:T(2,128)(2,1)S(1)} %copy-done.31, bf16[1,2,49,2880]{3,1,2,0:T(2,128)(2,1)S(1)} %get-tuple-element.28, pred[]{:T(512)S(6)} %eq.5, f32[3,2,49,2880]{3,2,1,0:T(8,128)} %copy-done.9, s32[]{:T(128)S(6)} %min.27, ...), kind=kOutput, calls=%fused_computation.34 | convolution fusion | flops 1630500480 | bytes 21197568 | tf_op jit(solution)/shard_map/dot_general | solution.py:25
  504.2 4.0 collective-permute-start.8
  519.6 12.2 %fusion.42 = bf16[2,49,2880]{2,1,0:T(8,128)(2,1)} fusion(bf16[1,2880,2880]{2,1,0:T(8,128)(2,1)} %all-gather.7.cloned.1.call-done, bf16[2,49,2880]{2,0,1:T(2,128)(2,1)S(1)} %collective-permute-done.8, bf16[1,2,49,2880]{3,1,2,0:T(2,128)(2,1)S(1)} %get-tuple-element.28, pred[]{:T(512)S(6)} %eq.5, f32[3,2,49,2880]{3,2,1,0:T(8,128)} %copy-done.9, s32[]{:T(128)S(6)} %min.26, ...), kind=kOutput, calls=%fused_computation.33 | convolution fusion | flops 1630500480 | bytes 21197568 | tf_op jit(solution)/shard_map/dot_general | solution.py:25
  533.4 4.1 collective-permute-start.9
  553.4 13.9 %bitcast_convert_fusion = bf16[2880,2880]{1,0:T(8,128)(2,1)} fusion(bf16[3,2,49,2880]{3,2,1,0:T(8,128)(2,1)} %bitcast_dynamic-update-slice_fusion.11, bf16[3,2,49,2880]{3,2,1,0:T(8,128)(2,1)S(1)} %bitcast_dynamic-update-slice_fusion.6), kind=kOutput, calls=%fused_computation.1 | convolution fusion | flops 4885401600 | bytes 19975680 | tf_op jit(solution)/shard_map/dot_general | solution.py:19
  567.3 249.9 %fusion.355 = (bf16[96,2880]{1,0:T(8,128)(2,1)S(1)}, bf16[96,360]{1,0:T(8,128)(2,1)S(1)}, bf16[96,360]{1,0:T(8,128)(2,1)S(1)}) fusion(bf16[2880,2880]{1,0:T(8,128)(2,1)} %bitcast_convert_fusion, bf16[2880,360]{1,0:T(8,128)(2,1)} %fusion.25, bf16[2880,360]{1,0:T(8,128)(2,1)S(1)} %copy-done.33), kind=kCustom, calls=%all-reduce-scatter.3 | all-reduce-scatter fusion | flops 11059201 | bytes 21427712
  819.3 5.6 collective-permute-start.11
  830.7 7.7 collective-permute-start.12
  838.3 18.2 %collective-permute-done.15 = bf16[90,360]{1,0:T(8,128)(2,1)S(1)} collective-permute-done((bf16[90,360]{1,0:T(8,128)(2,1)S(1)}, bf16[90,360]{1,0:T(8,128)(2,1)S(1)}, u32[]{:S(2)}, u32[]{:S(2)}) %collective-permute-start.15) | collective-permute-done | bytes 64832
  860.0 7.6 collective-permute-done.13
  869.1 9.5 %concatenate = bf16[282,2880]{1,0:T(8,128)(2,1)} concatenate(bf16[90,2880]{1,0:T(8,128)(2,1)S(1)} %collective-permute-done.11, bf16[96,2880]{1,0:T(8,128)(2,1)S(1)} %collective-permute-done.10, bf16[96,2880]{1,0:T(8,128)(2,1)S(1)} %get-tuple-element.15), dimensions={0} | concatenate | bytes 3248640
  (261 shorter events, 141.7 us)
Async XLA Ops:
  7.2 186.8 %all-gather.7.cloned.1.call-start = ((), (), s32[]{:S(2)}) async-start(), calls=%async_computation | async-start | bytes 19077120 | tf_op jit(solution)/shard_map/all_gather | solution.py:77
  7.9 240.7 %all-gather.9.cloned.1.call-start = ((), (), s32[]{:S(2)}) async-start(), calls=%async_computation.1 | async-start | bytes 2488320 | tf_op jit(solution)/shard_map/all_gather | solution.py:78
  8.7 294.7 %all-gather.11.cloned.1.call-start = ((), (), s32[]{:S(2)}) async-start(), calls=%async_computation.2 | async-start | bytes 2488320 | tf_op jit(solution)/shard_map/all_gather | solution.py:79
  306.4 11.1 %collective-permute-start = (bf16[2,49,2880]{2,0,1:T(2,128)(2,1)S(1)}, bf16[2,49,2880]{2,0,1:T(2,128)(2,1)S(1)}, u32[]{:S(2)}, u32[]{:S(2)}) collective-permute-start(bf16[2,49,2880]{2,0,1:T(2,128)(2,1)S(1)} %copy.44), channel_id=1, source_target_pairs={{0,32},{32,64},{64,96},{1,33},{33,65},{65,97},{2,34},{34,66},{66,9... | collective-permute-start | bytes 1693448 | tf_op jit(solution)/shard_map/ppermute | solution.py:10
  310.3 7.2 copy-start.17
  317.5 8.9 copy-start.2
  317.5 23.2 %slice-start = ((s8[16957440]{0:T(1024)(128)(4,1)}), s8[4194304]{0:T(1024)(128)(4,1)S(1)}, s32[]{:S(2)}) async-start(s8[16957440]{0:T(1024)(128)(4,1)} %bitcast.890), calls=%async_computation.3 | async-start | bytes 8388608
  317.5 23.2 %slice-start.1 = ((s8[16957440]{0:T(1024)(128)(4,1)}), s8[4194304]{0:T(1024)(128)(4,1)S(1)}, s32[]{:S(2)}) async-start(s8[16957440]{0:T(1024)(128)(4,1)} %bitcast.890), calls=%async_computation.4 | async-start | bytes 8388608
  317.5 23.2 %slice-start.2 = ((s8[16957440]{0:T(1024)(128)(4,1)}), s8[4194304]{0:T(1024)(128)(4,1)S(1)}, s32[]{:S(2)}) async-start(s8[16957440]{0:T(1024)(128)(4,1)} %bitcast.890), calls=%async_computation.5 | async-start | bytes 8388608
  326.4 14.4 %slice-start.3 = ((s8[16957440]{0:T(1024)(128)(4,1)}), s8[4194304]{0:T(1024)(128)(4,1)S(1)}, s32[]{:S(2)}) async-start(s8[16957440]{0:T(1024)(128)(4,1)} %bitcast.890), calls=%async_computation.6 | async-start | bytes 8388608
  329.7 11.1 %collective-permute-start.1 = (bf16[2,49,2880]{2,0,1:T(2,128)(2,1)S(1)}, bf16[2,49,2880]{2,0,1:T(2,128)(2,1)S(1)}, u32[]{:S(2)}, u32[]{:S(2)}) collective-permute-start(bf16[2,49,2880]{2,0,1:T(2,128)(2,1)S(1)} %copy.47), channel_id=1, source_target_pairs={{0,32},{32,64},{64,96},{1,33},{33,65},{65,97},{2,34},{34,66},{66,9... | collective-permute-start | bytes 1693448 | tf_op jit(solution)/shard_map/ppermute | solution.py:10
  331.6 9.1 %slice-start.4 = ((s8[16957440]{0:T(1024)(128)(4,1)}), s8[180224]{0:T(1024)(128)(4,1)S(1)}, s32[]{:S(2)}) async-start(s8[16957440]{0:T(1024)(128)(4,1)} %bitcast.890), calls=%async_computation.7 | async-start | bytes 360448
  346.7 11.1 %collective-permute-start.2 = (bf16[2,49,2880]{2,0,1:T(2,128)(2,1)S(1)}, bf16[2,49,2880]{2,0,1:T(2,128)(2,1)S(1)}, u32[]{:S(2)}, u32[]{:S(2)}) collective-permute-start(bf16[2,49,2880]{2,0,1:T(2,128)(2,1)S(1)} %copy.49), channel_id=1, source_target_pairs={{0,32},{32,64},{64,96},{1,33},{33,65},{65,97},{2,34},{34,66},{66,9... | collective-permute-start | bytes 1693448 | tf_op jit(solution)/shard_map/ppermute | solution.py:10
  363.7 11.1 %collective-permute-start.3 = (bf16[2,49,2880]{2,0,1:T(2,128)(2,1)S(1)}, bf16[2,49,2880]{2,0,1:T(2,128)(2,1)S(1)}, u32[]{:S(2)}, u32[]{:S(2)}) collective-permute-start(bf16[2,49,2880]{2,0,1:T(2,128)(2,1)S(1)} %copy.51), channel_id=1, source_target_pairs={{0,32},{32,64},{64,96},{1,33},{33,65},{65,97},{2,34},{34,66},{66,9... | collective-permute-start | bytes 1693448 | tf_op jit(solution)/shard_map/ppermute | solution.py:10
  379.9 11.2 %collective-permute-start.4 = (bf16[2,49,2880]{2,0,1:T(2,128)(2,1)S(1)}, bf16[2,49,2880]{2,0,1:T(2,128)(2,1)}, u32[]{:S(2)}, u32[]{:S(2)}) collective-permute-start(bf16[2,49,2880]{2,0,1:T(2,128)(2,1)S(1)} %copy.53), channel_id=1, source_target_pairs={{0,32},{32,64},{64,96},{1,33},{33,65},{65,97},{2,34},{34,66},{66,9... | collective-permute-start | bytes 1693448 | tf_op jit(solution)/shard_map/ppermute | solution.py:10
  385.1 10.9 %copy-start.15 = (bf16[1,2,49,2880]{3,1,2,0:T(2,128)(2,1)S(1)}, bf16[1,2,49,2880]{3,1,2,0:T(2,128)(2,1)}, u32[]{:S(2)}) copy-start(bf16[1,2,49,2880]{3,1,2,0:T(2,128)(2,1)} %get-tuple-element.30) | copy-start | bytes 1693444
  418.2 9.2 %collective-permute-start.5 = (bf16[2,49,2880]{2,0,1:T(2,128)(2,1)S(1)}, bf16[2,49,2880]{2,0,1:T(2,128)(2,1)S(1)}, u32[]{:S(2)}, u32[]{:S(2)}) collective-permute-start(bf16[2,49,2880]{2,0,1:T(2,128)(2,1)S(1)} %copy.57), channel_id=1, source_target_pairs={{32,0},{64,32},{96,64},{33,1},{65,33},{97,65},{34,2},{66,34},{98,6... | collective-permute-start | bytes 1693448 | tf_op jit(solution)/shard_map/ppermute | solution.py:10
  444.3 6.5 copy-start.20
  444.3 6.5 copy-start.25
  445.9 10.9 %collective-permute-start.6 = (bf16[2,49,2880]{2,0,1:T(2,128)(2,1)S(1)}, bf16[2,49,2880]{2,0,1:T(2,128)(2,1)S(1)}, u32[]{:S(2)}, u32[]{:S(2)}) collective-permute-start(bf16[2,49,2880]{2,0,1:T(2,128)(2,1)S(1)} %copy.60), channel_id=1, source_target_pairs={{32,0},{64,32},{96,64},{33,1},{65,33},{97,65},{34,2},{66,34},{98,6... | collective-permute-start | bytes 1693448 | tf_op jit(solution)/shard_map/ppermute | solution.py:10
  475.0 11.1 %collective-permute-start.7 = (bf16[2,49,2880]{2,0,1:T(2,128)(2,1)S(1)}, bf16[2,49,2880]{2,0,1:T(2,128)(2,1)S(1)}, u32[]{:S(2)}, u32[]{:S(2)}) collective-permute-start(bf16[2,49,2880]{2,0,1:T(2,128)(2,1)S(1)} %copy.62), channel_id=1, source_target_pairs={{32,0},{64,32},{96,64},{33,1},{65,33},{97,65},{34,2},{66,34},{98,6... | collective-permute-start | bytes 1693448 | tf_op jit(solution)/shard_map/ppermute | solution.py:10
  504.2 11.1 %collective-permute-start.8 = (bf16[2,49,2880]{2,0,1:T(2,128)(2,1)S(1)}, bf16[2,49,2880]{2,0,1:T(2,128)(2,1)S(1)}, u32[]{:S(2)}, u32[]{:S(2)}) collective-permute-start(bf16[2,49,2880]{2,0,1:T(2,128)(2,1)S(1)} %copy.64), channel_id=1, source_target_pairs={{32,0},{64,32},{96,64},{33,1},{65,33},{97,65},{34,2},{66,34},{98,6... | collective-permute-start | bytes 1693448 | tf_op jit(solution)/shard_map/ppermute | solution.py:10
  531.8 6.4 copy-start.29
  533.4 11.1 %collective-permute-start.9 = (bf16[2,49,2880]{2,0,1:T(2,128)(2,1)S(1)}, bf16[2,49,2880]{2,0,1:T(2,128)(2,1)S(1)}, u32[]{:S(2)}, u32[]{:S(2)}) collective-permute-start(bf16[2,49,2880]{2,0,1:T(2,128)(2,1)S(1)} %copy.66), channel_id=1, source_target_pairs={{32,0},{64,32},{96,64},{33,1},{65,33},{97,65},{34,2},{66,34},{98,6... | collective-permute-start | bytes 1693448 | tf_op jit(solution)/shard_map/ppermute | solution.py:10
  553.4 13.9 %copy-start.33 = (bf16[2880,360]{1,0:T(8,128)(2,1)S(1)}, bf16[2880,360]{1,0:T(8,128)(2,1)}, u32[]{:S(2)}) copy-start(bf16[2880,360]{1,0:T(8,128)(2,1)} %fusion.26) | copy-start | bytes 6220804
  567.3 262.1 %copy-start.44 = (u32[128]{0:T(128)S(1)}, u32[128]{0:T(128)}, u32[]{:S(2)}) copy-start(u32[128]{0:T(128)} %constant.371) | copy-start | bytes 1540
  817.2 51.9 %collective-permute-start.10 = (bf16[96,2880]{1,0:T(8,128)(2,1)S(1)}, bf16[96,2880]{1,0:T(8,128)(2,1)S(1)}, u32[]{:S(2)}, u32[]{:S(2)}) collective-permute-start(bf16[96,2880]{1,0:T(8,128)(2,1)S(1)} %get-tuple-element.15), channel_id=1, source_target_pairs={{0,1},{1,2},{2,3},{3,4},{4,5},{5,6},{6,7},{7,8},{8,9},{9,10},{10,1... | collective-permute-start | bytes 1658888
  819.3 49.8 %collective-permute-start.11 = (bf16[90,2880]{1,0:T(8,128)(2,1)S(1)}, bf16[90,2880]{1,0:T(8,128)(2,1)S(1)}, u32[]{:S(2)}, u32[]{:S(2)}) collective-permute-start(bf16[90,2880]{1,0:T(8,128)(2,1)S(1)} %slice.35), channel_id=1, source_target_pairs={{0,2},{1,3},{2,4},{3,5},{4,6},{5,7},{6,8},{7,9},{8,10},{9,11},{10,... | collective-permute-start | bytes 1555208
  824.9 33.6 %collective-permute-start.14 = (bf16[96,360]{1,0:T(8,128)(2,1)S(1)}, bf16[96,360]{1,0:T(8,128)(2,1)S(1)}, u32[]{:S(2)}, u32[]{:S(2)}) collective-permute-start(bf16[96,360]{1,0:T(8,128)(2,1)S(1)} %get-tuple-element.17), channel_id=1, source_target_pairs={{0,1},{1,2},{2,3},{3,4},{4,5},{5,6},{6,7},{7,8},{8,9},{9,10},{10,1... | collective-permute-start | bytes 207368
  826.8 29.7 %collective-permute-start.15 = (bf16[90,360]{1,0:T(8,128)(2,1)S(1)}, bf16[90,360]{1,0:T(8,128)(2,1)S(1)}, u32[]{:S(2)}, u32[]{:S(2)}) collective-permute-start(bf16[90,360]{1,0:T(8,128)(2,1)S(1)} %slice.37), channel_id=1, source_target_pairs={{0,2},{1,3},{2,4},{3,5},{4,6},{5,7},{6,8},{7,9},{8,10},{9,11},{10,... | collective-permute-start | bytes 194408
  830.7 36.9 %collective-permute-start.12 = (bf16[96,360]{1,0:T(8,128)(2,1)S(1)}, bf16[96,360]{1,0:T(8,128)(2,1)S(1)}, u32[]{:S(2)}, u32[]{:S(2)}) collective-permute-start(bf16[96,360]{1,0:T(8,128)(2,1)S(1)} %get-tuple-element.16), channel_id=1, source_target_pairs={{0,1},{1,2},{2,3},{3,4},{4,5},{5,6},{6,7},{7,8},{8,9},{9,10},{10,1... | collective-permute-start | bytes 207368
  856.5 11.0 %collective-permute-start.13 = (bf16[90,360]{1,0:T(8,128)(2,1)S(1)}, bf16[90,360]{1,0:T(8,128)(2,1)S(1)}, u32[]{:S(2)}, u32[]{:S(2)}) collective-permute-start(bf16[90,360]{1,0:T(8,128)(2,1)S(1)} %slice.36), channel_id=1, source_target_pairs={{0,2},{1,3},{2,4},{3,5},{4,6},{5,7},{6,8},{7,9},{8,10},{9,11},{10,... | collective-permute-start | bytes 194408
  (38 other events, 121.0 us)
Sparse Core Ops, SparseCore 0:
  10.3 183.6 all-gather.6
  196.3 52.3 all-gather.8
  251.0 52.3 all-gather.10
where the time goes:
time: 898 us; the launch traced here: 889 us
  waiting for transfers between devices  331 us (37%)
  blocking collectives  250 us (28%)
  matrix products  138 us (15%)
  local copies, waits for them, and re-layouts  65.1 us (7%)
  starting transfers between devices  50.5 us (6%)
  other arithmetic  38.4 us (4%)
  between operations  15.6 us (2%)
    unnamed x1, blocking collectives  250 us
    all_gather x1, waiting for transfers between devices, on_device(): lax.all_gather(weight[0], 'fsdp', axis=0, tiled=True)  168 us
    dot_general x17, matrix products, contract_cols(): lax.dot_general(left, right, (((1,), (1,)), ((), ())), preferred_element_...  74.6 us
    all_gather x1, waiting for transfers between devices, on_device(): lax.all_gather(excite[0], 'fsdp', axis=0, tiled=True)  52.7 us
    all_gather x1, waiting for transfers between devices, on_device(): lax.all_gather(squeeze[0], 'fsdp', axis=0, tiled=True)  45 us
    ppermute x10, waiting for transfers between devices, shifted(): lax.ppermute(value, axis, [(source, source + steps) for source in range(l...  37.7 us
    dot_general x6, matrix products, project(): result = jnp.dot(flat, matrix, preferred_element_type=jnp.float32)  34.4 us
    ppermute x10, starting transfers between devices, shifted(): lax.ppermute(value, axis, [(source, source + steps) for source in range(l...  28.8 us
  transfers between devices with their start and end apart: 19, of which 15 were waited for; matrix products, arithmetic and copies ran while one was open for 8% of the time, Pallas kernels for 0%

commit v1 on v0

v1 whole, which is shorter than its diff:
```python
import functools

import jax
import jax.numpy as jnp
from jax import lax
from jax.experimental import pallas as pl
from jax.experimental.pallas import tpu as pltpu
from jax.sharding import PartitionSpec as P

MESH = pl.DeviceIdType.MESH
F32, BF16 = jnp.float32, jnp.bfloat16
STEP = 16


def round_up(value, unit):
    return -(-value // unit) * unit


def sigmoid(value):
    return jax.nn.sigmoid(value)


def silu_slope(value):
    sigma = sigmoid(value)
    return sigma * (1.0 + value * (1.0 - sigma))


def dot_nn(left, right):
    return lax.dot_general(left, right, (((1,), (0,)), ((), ())), preferred_element_type=F32)


def dot_nt(left, right):
    return lax.dot_general(left, right, (((1,), (1,)), ((), ())), preferred_element_type=F32)


def dot_tn(left, right):
    return lax.dot_general(left, right, (((0,), (0,)), ((), ())), preferred_element_type=F32)


def pipeline_kernel(
    units, sections, pixels, width, hidden,
    w_ref, x_ref, g_ref,
    h, dh, pre, act, gate, pool, sq, hid, dsq, dex,
    part, mixed, from_a, from_b, second, full, grad, work,
    sq_buf, dq_buf,
    rs_send, rs_recv, ag_send, ag_recv, sq_send, sq_recv, dq_send, dq_recv, hop_send, hop_recv,
):
    rows = h.shape[1]
    cut = round_up(rows // 2, STEP)
    top, low = pl.ds(0, cut), pl.ds(cut, rows - cut)
    seg = lax.axis_index("segment")
    me = lax.axis_index("dp")
    near_a = me + 1 - 2 * lax.rem(me, 2)
    near_b = 3 - me
    far = lax.rem(me + 2, 4)
    after = lax.rem(seg + 1, sections)
    before = lax.rem(seg + sections - 1, sections)

    barrier = pltpu.get_barrier_semaphore()
    for target in ({"dp": near_a}, {"dp": near_b}, {"dp": far}, {"segment": after}, {"segment": before}):
        pl.semaphore_signal(barrier, inc=1, device_id=target, device_id_type=MESH)
    pl.semaphore_wait(barrier, 5)

    def remote(src, dst, send, recv, target):
        return pltpu.make_async_remote_copy(
            src_ref=src, dst_ref=dst, send_sem=send, recv_sem=recv, device_id=target, device_id_type=MESH
        )

    def columns(owner):
        return pl.ds(pl.multiple_of(owner * width, width), width)

    squeeze_cols = pl.ds(4 * width, hidden)
    excite_cols = pl.ds(4 * width + hidden, hidden)

    def chunk(index):
        return pl.ds(pl.multiple_of(index * STEP, STEP), STEP)

    def images(value):
        return value.reshape(STEP // 8, 8, value.shape[-1])

    def share(buf, sends, recvs, unit, value):
        buf[unit, me] = value
        copies = [
            remote(buf.at[unit, me], buf.at[unit, me], sends.at[unit, k], recvs.at[unit, k], {"dp": peer})
            for k, peer in enumerate((near_a, near_b, far))
        ]
        for copy in copies:
            copy.start()
        for copy in copies:
            copy.wait()
        return (buf[unit, 0] + buf[unit, 1]) + (buf[unit, 2] + buf[unit, 3])

    @pl.when(seg == 0)
    def _():
        h[...] = x_ref[...]

    @pl.when(seg == sections - 1)
    def _():
        dh[...] = x_ref[...]

    def hop_forward(unit):
        return remote(work.at[unit], h.at[unit], hop_send.at[unit], hop_recv.at[unit], {"segment": after})

    def hop_backward(unit):
        return remote(
            work.at[units + unit], dh.at[unit], hop_send.at[units + unit], hop_recv.at[units + unit], {"segment": before}
        )

    def forward(unit, carry):
        @pl.when(seg > 0)
        def _():
            hop_forward(unit).wait_recv()

        def piece(slot, owner):
            part[unit, slot] = dot_nn(h[unit], w_ref[:, columns(owner)]).astype(BF16)

        def reduce_copy(k, src, dst, target):
            return remote(src, dst, rs_send.at[unit, k], rs_recv.at[unit, k], {"dp": target})

        piece(0, far)
        far_a = reduce_copy(0, part.at[unit, 0, top], from_a.at[unit, 1], near_a)
        far_b = reduce_copy(1, part.at[unit, 0, low], from_b.at[unit, 1], near_b)
        far_a.start()
        far_b.start()
        piece(1, near_a)
        own_a = reduce_copy(2, part.at[unit, 1, top], from_a.at[unit, 0], near_a)
        own_a.start()
        piece(2, near_b)
        own_b = reduce_copy(3, part.at[unit, 2, low], from_b.at[unit, 0], near_b)
        own_b.start()
        pre[unit] = dot_nn(h[unit], w_ref[:, columns(me)])

        far_a.wait_recv()

        @pl.loop(0, cut // STEP)
        def _(i):
            total = part[unit, 2, chunk(i)].astype(F32) + from_a[unit, 1, chunk(i)].astype(F32)
            mixed[unit, chunk(i)] = total.astype(BF16)

        mix_b = reduce_copy(4, mixed.at[unit, top], second.at[unit, top], near_b)
        mix_b.start()
        far_b.wait_recv()

        @pl.loop(0, (rows - cut) // STEP)
        def _(i):
            there = pl.ds(pl.multiple_of(cut + i * STEP, STEP), STEP)
            total = part[unit, 1, there].astype(F32) + from_b[unit, 1, chunk(i)].astype(F32)
            mixed[unit, there] = total.astype(BF16)

        mix_a = reduce_copy(5, mixed.at[unit, low], second.at[unit, low], near_a)
        mix_a.start()
        own_a.wait_recv()
        own_b.wait_recv()

        def finish(source, offset, i, sums):
            there = pl.ds(pl.multiple_of(offset + i * STEP, STEP), STEP)
            total = pre[unit, there] + source[unit, 0, chunk(i)].astype(F32) + second[unit, there].astype(F32)
            pre[unit, there] = total
            active = (total * sigmoid(total)).astype(BF16)
            act[unit, there] = active
            return sums + jnp.sum(images(active.astype(F32)), axis=0)

        mix_b.wait_recv()
        sums = lax.fori_loop(0, cut // STEP, functools.partial(finish, from_a, 0), jnp.zeros((8, width), F32))
        mix_a.wait_recv()
        sums = lax.fori_loop(0, (rows - cut) // STEP, functools.partial(finish, from_b, cut), sums)
        pooled = (sums / pixels).astype(BF16)
        pool[unit] = pooled.astype(F32)
        squeezed = share(sq_buf, sq_send, sq_recv, unit, dot_nn(pooled, w_ref[:, squeeze_cols]))
        hidden_now = (squeezed * sigmoid(squeezed)).astype(BF16)
        sq[unit] = squeezed
        hid[unit] = hidden_now.astype(F32)
        gates = sigmoid(dot_nt(hidden_now, w_ref[:, excite_cols]))
        gate[unit] = gates

        @pl.when(seg < sections - 1)
        def _():
            @pl.loop(0, rows // STEP)
            def _(i):
                scaled = images(act[unit, chunk(i)].astype(F32)) * gates
                total = h[unit, chunk(i)].astype(F32) + scaled.reshape(STEP, width)
                work[unit, chunk(i)] = total.astype(BF16)

            hop_forward(unit).start()

        for copy in (far_a, far_b, own_a, own_b, mix_b, mix_a):
            copy.wait_send()
        return carry

    lax.fori_loop(0, units, forward, 0)

    grad[...] = jnp.zeros_like(grad)

    def backward(unit, carry):
        @pl.when(seg < sections - 1)
        def _():
            hop_backward(unit).wait_recv()

        def weigh(i, sums):
            product = dh[unit, chunk(i)].astype(F32) * act[unit, chunk(i)].astype(F32)
            return sums + jnp.sum(images(product), axis=0)

        d_gate = lax.fori_loop(0, rows // STEP, weigh, jnp.zeros((8, width), F32))
        gates = gate[unit]
        d_excite = (d_gate * gates * (1.0 - gates)).astype(BF16)
        dex[unit] = d_excite.astype(F32)
        d_hidden = share(dq_buf, dq_send, dq_recv, unit, dot_nn(d_excite, w_ref[:, excite_cols]))
        d_squeezed = (d_hidden * silu_slope(sq[unit])).astype(BF16)
        dsq[unit] = d_squeezed.astype(F32)
        d_pool = dot_nt(d_squeezed, w_ref[:, squeeze_cols]) / pixels

        @pl.loop(0, rows // STEP)
        def _(i):
            d_act = images(dh[unit, chunk(i)].astype(F32)) * gates + d_pool
            d_pre = d_act * silu_slope(images(pre[unit, chunk(i)]))
            full[unit, 0, chunk(i)] = d_pre.reshape(STEP, width).astype(BF16)

        def gather_copy(k, src, dst, target):
            return remote(src, dst, ag_send.at[unit, k], ag_recv.at[unit, k], {"dp": target})

        own_a = gather_copy(0, full.at[unit, 0], full.at[unit, 1], near_a)
        own_b = gather_copy(1, full.at[unit, 0], full.at[unit, 2], near_b)
        pass_b = gather_copy(2, full.at[unit, 1, top], full.at[unit, 3, top], near_b)
        pass_a = gather_copy(3, full.at[unit, 2, low], full.at[unit, 3, low], near_a)
        own_a.start()
        own_b.start()

        def back(slot, owner):
            return dot_nt(full[unit, slot], w_ref[:, columns(owner)])

        @pl.when(seg > 0)
        def _():
            pre[unit] = back(0, me) + dh[unit].astype(F32)

        own_a.wait_recv()
        pass_b.start()
        own_b.wait_recv()
        pass_a.start()

        @pl.when(seg > 0)
        def _():
            pre[unit] += back(1, near_a)
            pre[unit] += back(2, near_b)

        pass_b.wait_recv()
        pass_a.wait_recv()

        @pl.when(seg > 0)
        def _():
            work[units + unit] = (pre[unit] + back(3, far)).astype(BF16)
            hop_backward(unit).start()

        for slot in range(4):
            grad[slot] += dot_tn(h[unit], full[unit, slot])
        for copy in (own_a, own_b, pass_b, pass_a):
            copy.wait_send()
        return carry

    lax.fori_loop(0, units, backward, 0)

    for slot, owner in enumerate((me, near_a, near_b, far)):
        g_ref[:, columns(owner)] = grad[slot].astype(BF16)

    def stacked(ref):
        return ref[...].reshape(units * 8, ref.shape[-1]).astype(BF16)

    g_ref[:, squeeze_cols] = dot_tn(stacked(pool), stacked(dsq)).astype(BF16)
    g_ref[:, excite_cols] = dot_tn(stacked(dex), stacked(hid)).astype(BF16)

    @pl.when(seg < sections - 1)
    def _():
        for unit in range(units):
            hop_forward(unit).wait_send()

    @pl.when(seg > 0)
    def _():
        for unit in range(units):
            hop_backward(unit).wait_send()


def run_pipeline(weights, x, sections, pixels, hidden):
    units, rows, width = x.shape
    cut = round_up(rows // 2, STEP)
    vmem, dma = pltpu.VMEM, pltpu.SemaphoreType.DMA
    return pl.pallas_call(
        functools.partial(pipeline_kernel, units, sections, pixels, width, hidden),
        out_shape=jax.ShapeDtypeStruct(weights.shape, BF16),
        in_specs=[pl.BlockSpec(memory_space=pltpu.VMEM)] * 2,
        out_specs=pl.BlockSpec(memory_space=pltpu.VMEM),
        scratch_shapes=[
            vmem((units, rows, width), BF16),
            vmem((units, rows, width), BF16),
            vmem((units, rows, width), F32),
            vmem((units, rows, width), BF16),
            vmem((units, 8, width), F32),
            vmem((units, 8, width), F32),
            vmem((units, 8, hidden), F32),
            vmem((units, 8, hidden), F32),
            vmem((units, 8, hidden), F32),
            vmem((units, 8, width), F32),
            vmem((units, 3, rows, width), BF16),
            vmem((units, rows, width), BF16),
            vmem((units, 2, cut, width), BF16),
            vmem((units, 2, rows - cut, width), BF16),
            vmem((units, rows, width), BF16),
            vmem((units, 4, rows, width), BF16),
            vmem((4, width, width), F32),
            vmem((2 * units, rows, width), BF16),
            vmem((units, 4, 8, hidden), F32),
            vmem((units, 4, 8, hidden), F32),
            dma((units, 6)), dma((units, 6)),
            dma((units, 4)), dma((units, 4)),
            dma((units, 3)), dma((units, 3)),
            dma((units, 3)), dma((units, 3)),
            dma((2 * units,)), dma((2 * units,)),
        ],
        compiler_params=pltpu.CompilerParams(
            collective_id=0, has_side_effects=True, vmem_limit_bytes=67_000_000
        ),
        name="pipeline",
    )(weights, x)


def spread(value, parts, sets, piece, run):
    lead = value.shape[:-1]
    split = value.reshape(lead + (parts, sets, piece))
    split = jnp.pad(split, [(0, 0)] * (len(lead) + 2) + [(0, run - piece)])
    return jnp.swapaxes(split, -3, -2).reshape(lead + (sets, parts * run))


def gathered(value, parts, sets, piece, run):
    lead = value.shape[:-1]
    split = jnp.swapaxes(value.reshape(lead + (sets, parts, run)), -3, -2)[..., :piece]
    return split.reshape(lead + (parts * sets * piece,))


def on_device(inputs, cotangent, plan, weight, squeeze, excite):
    sections, parts, sets = (lax.axis_size(name) for name in ("segment", "fsdp", "dp"))
    units, each, pixels, channels = inputs.shape
    piece = channels // (parts * sets)
    run = round_up(piece, 16)
    hidden_real = squeeze.shape[-1]
    hidden = round_up(hidden_real, 128)
    me = lax.axis_index("dp")

    def rows_of(array):
        return lax.dynamic_slice_in_dim(array[0], me * piece, piece, axis=0)

    own_w = spread(rows_of(weight), parts, sets, piece, run).reshape(piece, -1)
    own = jnp.concatenate(
        [
            own_w,
            jnp.pad(rows_of(squeeze), ((0, 0), (0, hidden - hidden_real))),
            jnp.pad(rows_of(excite), ((0, 0), (0, hidden - hidden_real))),
        ],
        axis=1,
    )
    own = jnp.pad(own, ((0, run - piece), (0, 0)))
    weights = lax.all_gather(own, "fsdp", axis=0, tiled=True)

    last = lax.axis_index("segment") == sections - 1
    x = jnp.where(last, cotangent, inputs[plan])
    x = spread(x, parts, sets, piece, run)
    x = lax.all_to_all(x, "dp", split_axis=3, concat_axis=0, tiled=False)
    x = x.transpose(1, 3, 0, 2, 4)
    x = jnp.pad(x, ((0, 0), (0, pixels % 2), (0, 0), (0, 0), (0, 0)))
    x = x.reshape(units, -1, x.shape[-1])

    grads = run_pipeline(weights, x, sections, pixels, hidden)
    mine = lax.psum_scatter(grads, "fsdp", scatter_dimension=0, tiled=True)[:piece]
    width = parts * run
    grad_w = gathered(mine[:, : sets * width].astype(F32), parts, sets, piece, run)
    grad_s = mine[:, sets * width :][:, :hidden_real].astype(F32)
    grad_e = mine[:, sets * width + hidden :][:, :hidden_real].astype(F32)
    return (grad_w[None], grad_s[None], grad_e[None])


def solution(mesh):
    data = P(None, ("fsdp", "dp"), None, None)
    owned = P("segment", "fsdp", None)
    result = P("segment", ("fsdp", "dp"), None)
    return jax.shard_map(
        on_device,
        mesh=mesh,
        in_specs=(data, data, P(), owned, owned, owned),
        out_specs=(result,) * 3,
        check_vma=False,
    )
```

time: 898 us -> 541 us (0.60)
  the two profiles are of different devices: /device:TPU:42 before, /device:TPU:0 now
where the time goes in v1:
time: 541 us; the launch traced here: 540 us
  Pallas kernels  329 us (61%)
  waiting for transfers between devices  120 us (22%)
  local copies, waits for them, and re-layouts  44.6 us (8%)
  blocking collectives  27.8 us (5%)
  between operations  14.2 us (3%)
    pallas_call x1, Pallas kernels, run_pipeline(): pl.pallas_call(functools.partial(pipeline_kernel, units, sections, pixels...  329 us
    reduce_scatter x1, waiting for transfers between devices, on_device(): lax.psum_scatter(grads, 'fsdp', scatter_dimension=0, tiled=True)[:piece]  92.4 us
    all_to_all x1, blocking collectives, on_device(): x = lax.all_to_all(x, 'dp', split_axis=3, concat_axis=0, tiled=False)  27.8 us
    all_gather x1, waiting for transfers between devices, on_device(): weights = lax.all_gather(own, 'fsdp', axis=0, tiled=True)  27.4 us
    reshape x2, local copies, waits for them, and re-layouts, spread(): split = value.reshape(lead + (parts, sets, piece))  14.2 us
  transfers between devices with their start and end apart: 2, of which 2 were waited for; matrix products, arithmetic and copies ran while one was open for 6% of the time, Pallas kernels for 0%

profile of v1, /device:TPU:0, one launch (start us, length us, event | category | flops | bytes accessed | tf_op | source)
XLA Modules:
  0.0 540.5 jit_solution(3524601866497915425)
XLA Ops:
  7.2 0.0 all-gather.2.cloned.1.call-start
  7.2 1.2 constant_dynamic-slice_fusion
  8.4 2.5 reshape.24
  10.9 0.4 pad_bitcast_fusion.1
  11.3 0.1 copy.18
  11.5 1.0 reshape_reshape.3
  12.5 1.0 dynamic-slice_bitcast_fusion
  13.5 0.1 fusion.4
  13.6 0.9 pad.26
  14.5 0.2 reduce-scatter.2.cloned.1.call-start
  14.8 0.4 copy-done
  15.2 5.8 %gather_fusion = bf16[3,2,49,2880]{3,1,2,0:T(2,128)(2,1)S(1)} fusion(bf16[3,2,49,2880]{3,1,2,0:T(2,128)(2,1)S(1)} %copy-done, s32[1024]{0:T(1024)S(1)} %pad_clamp_fusion), kind=kCustom, calls=%fused_computation | custom fusion | bytes 3386892 | tf_op jit(solution)/shard_map/gather | solution.py:362
  21.1 3.1 broadcast_select_fusion
  24.1 11.7 %reshape.25 = bf16[3,2,49,8,4,90]{5,4,3,1,2,0:T(4,128)(2,1)S(1)} reshape(bf16[3,2,49,2880]{3,1,2,0:T(2,128)(2,1)} %broadcast_select_fusion) | data formatting | bytes 3386880 | tf_op jit(solution)/shard_map/reshape | solution.py:326
  35.9 1.5 pad_bitcast_fusion
  37.3 0.3 copy.19
  37.7 4.9 broadcast_in_dim_reshape.9
  42.6 27.8 %all_to_all.15 = bf16[1,3,2,49,4,768]{5,2,3,1,0,4:T(2,128)(2,1)S(1)} all-to-all(bf16[1,3,2,49,4,768]{5,2,3,1,0,4:T(2,128)(2,1)} %broadcast_in_dim_reshape.9), channel_id=1, replica_groups=mesh['segment'=4,'fsdp'=8,'dp'=4] {'dp'}, dimensions={4} | all-to-all | bytes 3612672 | tf_op jit(solution)/shard_map/all_to_all | solution.py:364
  70.4 1.2 copy.24
  71.6 1.4 pad.28.clone
  73.0 2.2 reshape.26.x_ref
  75.2 27.4 %all-gather.2.cloned.1.call-done.w_ref = bf16[768,3840]{1,0:T(8,128)(2,1)} async-done(((bf16[96,3840]{1,0:T(8,128)(2,1)}), bf16[768,3840]{1,0:T(8,128)(2,1)}) %all-gather.2.cloned.1.call-update) | async-done | bytes 5898256 | tf_op jit(solution)/shard_map/all_gather | solution.py:359
  102.6 329.5 %pipeline.1 = bf16[768,3840]{1,0:T(8,128)(2,1)} custom-call(bf16[768,3840]{1,0:T(8,128)(2,1)} %all-gather.2.cloned.1.call-done.w_ref, bf16[3,400,768]{2,1,0:T(8,128)(2,1)} %reshape.26.x_ref), custom_call_target="tpu_custom_call" | custom-call | tf_op jit(solution)/shard_map/pipeline/pallas_call | solution.py:285
  432.1 92.4 %reduce-scatter.2.cloned.1.call-done = bf16[96,3840]{1,0:T(8,128)(2,1)} async-done(((bf16[768,3840]{1,0:T(8,128)(2,1)}), bf16[96,3840]{1,0:T(8,128)(2,1)}) %reduce-scatter.2.cloned.1.call-update) | async-done | bytes 737296 | tf_op jit(solution)/shard_map/reduce_scatter | solution.py:370
  524.6 0.9 fusion.5
  525.5 0.8 copy.23
  526.3 0.8 copy.22
  527.1 1.1 slice.27
  528.2 0.7 reshape.27
  529.0 0.2 slice_convert_fusion
  529.2 0.4 copy.21
  529.6 4.1 reshape.28
  (7 shorter events, 0.1 us)
Async XLA Ops:
  7.2 95.5 %all-gather.2.cloned.1.call-start = ((), (), s32[]{:S(2)}) async-start(), calls=%async_computation.2 | async-start | bytes 6635520 | tf_op jit(solution)/shard_map/all_gather | solution.py:359
  13.5 1.3 copy-start.1
  13.5 1.7 copy-start
  14.5 510.1 %reduce-scatter.2.cloned.1.call-start = ((), (), s32[]{:S(2)}) async-start(), calls=%async_computation.3 | async-start | bytes 6635520 | tf_op jit(solution)/shard_map/reduce_scatter | solution.py:370
Sparse Core Ops, SparseCore 0:
  14.6 87.9 all-gather.1
  432.3 92.2 reduce-scatter.1
